TPU v7x, 32 devices: a whole 2x2x4 slice. The times are simulated.
32 devices in a mesh: dp: 4 (over y, x), tensor: 8 (over z, core).
Axes of the slice: x: 2, y: 2, z: 4, core: 2. Of those that a mesh axis runs over, the one named last changes fastest.
Arguments:
- latents: bfloat16 [4, 2048, 1152], P('dp', 'tensor'), may hold values from -6 to 6
- conditioning: bfloat16 [4, 1152], P('dp', 'tensor'), may hold values from -6 to 6
- ada_weight: bfloat16 [2, 1152, 6912], P(None, 'tensor'), may hold values from -0.1875 to 0.1875
- ada_bias: bfloat16 [2, 6912], replicated, may hold values from -3 to 3
- qkv_weight: bfloat16 [2, 1152, 3, 1152], P(None, None, None, 'tensor'), may hold values from -0.1875 to 0.1875
- qkv_bias: bfloat16 [2, 2, 1152], P(None, None, 'tensor'), may hold values from -3 to 3
- out_weight: bfloat16 [2, 1152, 1152], P(None, 'tensor'), may hold values from -0.75 to 0.75
- out_bias: bfloat16 [2, 1152], replicated, may hold values from -3 to 3
- fc1_weight: bfloat16 [2, 1152, 4608], P(None, None, 'tensor'), may hold values from -0.1875 to 0.1875
- fc1_bias: bfloat16 [2, 4608], P(None, 'tensor'), may hold values from -3 to 3
- fc2_weight: bfloat16 [2, 4608, 1152], P(None, 'tensor'), may hold values from -0.09375 to 0.09375
- fc2_bias: bfloat16 [2, 1152], replicated, may hold values from -3 to 3
- out_grad: bfloat16 [4, 2048, 1152], P('dp', 'tensor'), may hold values from -6 to 6
Outputs:
- layer_output: bfloat16 [4, 2048, 1152], P('dp', 'tensor')
- latents_grad: bfloat16 [4, 2048, 1152], P('dp', 'tensor')
- conditioning_grad: bfloat16 [4, 1152], P('dp', 'tensor')
- ada_weight_grad: float32 [2, 1152, 6912], P(None, 'tensor')
- ada_bias_grad: float32 [2, 6912], replicated
- qkv_weight_grad: float32 [2, 1152, 3, 1152], P(None, None, None, 'tensor')
- qkv_bias_grad: float32 [2, 2, 1152], P(None, None, 'tensor')
- out_weight_grad: float32 [2, 1152, 1152], P(None, 'tensor')
- out_bias_grad: float32 [2, 1152], replicated
- fc1_weight_grad: float32 [2, 1152, 4608], P(None, None, 'tensor')
- fc1_bias_grad: float32 [2, 4608], P(None, 'tensor')
- fc2_weight_grad: float32 [2, 4608, 1152], P(None, 'tensor')
- fc2_bias_grad: float32 [2, 1152], replicated
All inputs are finite; a program needn't handle non-finite values.
Results may differ from a plain program's by a relative error of at most 0.04.
Values may be sent and summed in bfloat16 or wider, within the bound.
A program may use at most 256 MiB of HBM per device.

v0:
```python
from functools import partial
import jax
import jax.numpy as jnp
from jax import lax
from jax.sharding import PartitionSpec as P

HEAD_DIM = 72
PATCHES = 256
FRAMES = 8
LAYERS = 2


def normalize(stream):
    centered = stream - jnp.mean(stream, axis=-1, keepdims=True)
    variance = jnp.mean(centered * centered, axis=-1, keepdims=True)
    return centered * lax.rsqrt(variance + 1e-06)


def modulate(stream, shift_in, scale_in):
    return normalize(stream) * (1.0 + scale_in) + shift_in


def grouped(token_rows, spatial):
    heads_here = token_rows.shape[1] // HEAD_DIM
    shaped = token_rows.reshape(FRAMES, PATCHES, heads_here, HEAD_DIM)
    if spatial:
        return shaped
    return jnp.transpose(shaped, (1, 0, 2, 3))


def ungrouped(groups, spatial):
    if not spatial:
        groups = jnp.transpose(groups, (1, 0, 2, 3))
    return groups.reshape(FRAMES * PATCHES, groups.shape[2] * HEAD_DIM)


def softmax_rows(query_g, key_g):
    scores = jnp.einsum(
        "gqhd,gkhd->ghqk", query_g, key_g, preferred_element_type=jnp.float32
    ) * HEAD_DIM ** (-0.5)
    return jax.nn.softmax(scores, axis=-1)


def attend(query_rows, key_rows, value_rows, spatial):
    attn_probs = softmax_rows(grouped(query_rows, spatial), grouped(key_rows, spatial)).astype(
        jnp.bfloat16
    )
    mixed = jnp.einsum(
        "ghqk,gkhd->gqhd",
        attn_probs,
        grouped(value_rows, spatial),
        preferred_element_type=jnp.float32,
    )
    return ungrouped(mixed, spatial)


def attend_back(query_rows, key_rows, value_rows, mixed_grad, spatial):
    query_g = grouped(query_rows, spatial)
    key_g = grouped(key_rows, spatial)
    value_g = grouped(value_rows, spatial)
    grad_g = grouped(mixed_grad, spatial)
    probs_full = softmax_rows(query_g, key_g)
    value_grad = jnp.einsum(
        "ghqk,gqhd->gkhd",
        probs_full.astype(jnp.bfloat16),
        grad_g,
        preferred_element_type=jnp.float32,
    )
    probs_grad = jnp.einsum("gqhd,gkhd->ghqk", grad_g, value_g, preferred_element_type=jnp.float32)
    score_grad = probs_full * (
        probs_grad - jnp.sum(probs_grad * probs_full, axis=-1, keepdims=True)
    )
    score_low = score_grad.astype(jnp.bfloat16)
    factor = HEAD_DIM ** (-0.5)
    query_grad = (
        jnp.einsum("ghqk,gkhd->gqhd", score_low, key_g, preferred_element_type=jnp.float32) * factor
    )
    key_grad = (
        jnp.einsum("ghqk,gqhd->gkhd", score_low, query_g, preferred_element_type=jnp.float32)
        * factor
    )
    return (
        ungrouped(query_grad, spatial),
        ungrouped(key_grad, spatial),
        ungrouped(value_grad, spatial),
    )


def spread_rows(row_block):
    return lax.all_gather(row_block, "tensor", axis=0, tiled=True)


def reduce_rows(partial_terms):
    return lax.psum_scatter(
        partial_terms.astype(jnp.bfloat16), "tensor", scatter_dimension=0, tiled=True
    ).astype(jnp.float32)


def spread_grads(row_block):
    return lax.all_gather(row_block, "tensor", axis=0, tiled=True)


def reduce_grads(partial_terms):
    return lax.psum_scatter(
        partial_terms.astype(jnp.bfloat16), "tensor", scatter_dimension=0, tiled=True
    ).astype(jnp.float32)


def layer_forward(stream, modulation, params, spatial):
    qkv_w, qkv_b, out_w, out_b, fc1_w, fc1_b, fc2_w, fc2_b = params
    shift_att, scale_att, gate_att, shift_mlp, scale_mlp, gate_mlp = jnp.split(modulation, 6)
    normed = spread_rows(modulate(stream, shift_att, scale_att).astype(jnp.bfloat16))
    head_width = qkv_w.shape[2]
    projected = jnp.dot(
        normed, qkv_w.reshape(qkv_w.shape[0], 3 * head_width), preferred_element_type=jnp.float32
    )
    query_rows = (projected[:, :head_width] + qkv_b[0].astype(jnp.float32)).astype(jnp.bfloat16)
    key_rows = projected[:, head_width : 2 * head_width].astype(jnp.bfloat16)
    value_rows = (projected[:, 2 * head_width :] + qkv_b[1].astype(jnp.float32)).astype(
        jnp.bfloat16
    )
    heads_out = attend(query_rows, key_rows, value_rows, spatial).astype(jnp.bfloat16)
    attn_branch = reduce_rows(
        jnp.dot(heads_out, out_w, preferred_element_type=jnp.float32)
    ) + out_b.astype(jnp.float32)
    middle = stream + gate_att * attn_branch
    normed_mlp = spread_rows(modulate(middle, shift_mlp, scale_mlp).astype(jnp.bfloat16))
    hidden = jnp.dot(normed_mlp, fc1_w, preferred_element_type=jnp.float32) + fc1_b.astype(
        jnp.float32
    )
    activated = jax.nn.gelu(hidden, approximate=True).astype(jnp.bfloat16)
    mlp_branch = reduce_rows(
        jnp.dot(activated, fc2_w, preferred_element_type=jnp.float32)
    ) + fc2_b.astype(jnp.float32)
    result = middle + gate_mlp * mlp_branch
    saved = (
        normed,
        query_rows,
        key_rows,
        value_rows,
        heads_out,
        attn_branch,
        middle,
        normed_mlp,
        hidden,
        mlp_branch,
    )
    return (result, saved)


def layer_backward(stream, modulation, params, saved, stream_grad, spatial):
    qkv_w, qkv_b, out_w, out_b, fc1_w, fc1_b, fc2_w, fc2_b = params
    (
        normed,
        query_rows,
        key_rows,
        value_rows,
        heads_out,
        attn_branch,
        middle,
        normed_mlp,
        hidden,
        mlp_branch,
    ) = saved
    shift_att, scale_att, gate_att, shift_mlp, scale_mlp, gate_mlp = jnp.split(modulation, 6)
    head_width = qkv_w.shape[2]
    mlp_grad = (gate_mlp * stream_grad).astype(jnp.bfloat16)
    gate_mlp_grad = jnp.sum(stream_grad * mlp_branch, axis=0)
    fc2_b_grad = jnp.sum(mlp_grad, axis=0, dtype=jnp.float32)
    mlp_grad_all = spread_grads(mlp_grad)
    gelu_out, gelu_back = jax.vjp(partial(jax.nn.gelu, approximate=True), hidden)
    activated = gelu_out.astype(jnp.bfloat16)
    fc2_w_grad = jnp.einsum(
        "tf,td->fd", activated, mlp_grad_all, preferred_element_type=jnp.float32
    )
    act_grad = jnp.einsum("td,fd->tf", mlp_grad_all, fc2_w, preferred_element_type=jnp.float32)
    hidden_grad = gelu_back(act_grad)[0].astype(jnp.bfloat16)
    fc1_b_grad = jnp.sum(hidden_grad, axis=0, dtype=jnp.float32)
    fc1_w_grad = jnp.einsum(
        "td,tf->df", normed_mlp, hidden_grad, preferred_element_type=jnp.float32
    )
    mlp_in_grad = reduce_grads(
        jnp.einsum("tf,df->td", hidden_grad, fc1_w, preferred_element_type=jnp.float32)
    )
    _, mlp_norm_back = jax.vjp(modulate, middle, shift_mlp, scale_mlp)
    middle_part, shift_mlp_grad, scale_mlp_grad = mlp_norm_back(mlp_in_grad)
    middle_grad = stream_grad + middle_part
    attn_grad = (gate_att * middle_grad).astype(jnp.bfloat16)
    gate_att_grad = jnp.sum(middle_grad * attn_branch, axis=0)
    out_b_grad = jnp.sum(attn_grad, axis=0, dtype=jnp.float32)
    attn_grad_all = spread_grads(attn_grad)
    out_w_grad = jnp.einsum(
        "tw,td->wd", heads_out, attn_grad_all, preferred_element_type=jnp.float32
    )
    heads_grad = jnp.einsum(
        "td,wd->tw", attn_grad_all, out_w, preferred_element_type=jnp.float32
    ).astype(jnp.bfloat16)
    query_grad, key_grad, value_grad = attend_back(
        query_rows, key_rows, value_rows, heads_grad, spatial
    )
    qkv_grad = jnp.concatenate([query_grad, key_grad, value_grad], axis=1).astype(jnp.bfloat16)
    qkv_b_grad = jnp.stack(
        [
            jnp.sum(qkv_grad[:, :head_width], axis=0, dtype=jnp.float32),
            jnp.sum(qkv_grad[:, 2 * head_width :], axis=0, dtype=jnp.float32),
        ]
    )
    qkv_flat = qkv_w.reshape(qkv_w.shape[0], 3 * head_width)
    qkv_w_grad = jnp.einsum(
        "td,tw->dw", normed, qkv_grad, preferred_element_type=jnp.float32
    ).reshape(qkv_w.shape)
    attn_in_grad = reduce_grads(
        jnp.einsum("tw,dw->td", qkv_grad, qkv_flat, preferred_element_type=jnp.float32)
    )
    _, att_norm_back = jax.vjp(modulate, stream, shift_att, scale_att)
    stream_part, shift_att_grad, scale_att_grad = att_norm_back(attn_in_grad)
    input_grad = middle_grad + stream_part
    modulation_grad = jnp.concatenate(
        [
            shift_att_grad,
            scale_att_grad,
            gate_att_grad,
            shift_mlp_grad,
            scale_mlp_grad,
            gate_mlp_grad,
        ]
    )
    return (
        input_grad,
        modulation_grad,
        (
            qkv_w_grad,
            qkv_b_grad,
            out_w_grad,
            out_b_grad,
            fc1_w_grad,
            fc1_b_grad,
            fc2_w_grad,
            fc2_b_grad,
        ),
    )


def per_device(
    latents,
    conditioning,
    ada_weight,
    ada_bias,
    qkv_weight,
    qkv_bias,
    out_weight,
    out_bias,
    fc1_weight,
    fc1_bias,
    fc2_weight,
    fc2_bias,
    out_grad,
):
    cond_row = conditioning[0].astype(jnp.float32)
    silu_out, silu_back = jax.vjp(jax.nn.silu, cond_row)
    silu_cond = silu_out.astype(jnp.bfloat16)
    ada_terms = jnp.einsum("d,ldm->lm", silu_cond, ada_weight, preferred_element_type=jnp.float32)
    modulations = lax.psum(ada_terms, "tensor") + ada_bias.astype(jnp.float32)
    stacked = (
        qkv_weight,
        qkv_bias,
        out_weight,
        out_bias,
        fc1_weight,
        fc1_bias,
        fc2_weight,
        fc2_bias,
    )
    stream = latents[0].astype(jnp.float32)
    inputs_kept = []
    saved_all = []
    for layer_idx in range(LAYERS):
        params = tuple((member[layer_idx] for member in stacked))
        inputs_kept.append(stream)
        stream, saved = layer_forward(stream, modulations[layer_idx], params, layer_idx % 2 == 0)
        saved_all.append(saved)
    layer_output = stream.astype(jnp.bfloat16)[None]
    stream_grad = out_grad[0].astype(jnp.float32)
    mod_grads = [None] * LAYERS
    layer_grads = [None] * LAYERS
    for layer_idx in reversed(range(LAYERS)):
        params = tuple((member[layer_idx] for member in stacked))
        spatial = layer_idx % 2 == 0
        saved = layer_forward(inputs_kept[layer_idx], modulations[layer_idx], params, spatial)[1]
        stream_grad, mod_grads[layer_idx], layer_grads[layer_idx] = layer_backward(
            inputs_kept[layer_idx], modulations[layer_idx], params, saved, stream_grad, spatial
        )

    def collect(position):
        return jnp.stack([member[position] for member in layer_grads])

    mod_sum, out_b_sum, fc2_b_sum = (
        lax.psum(jnp.stack(mod_grads).astype(jnp.bfloat16), "tensor").astype(jnp.float32),
        lax.psum(collect(3).astype(jnp.bfloat16), "tensor").astype(jnp.float32),
        lax.psum(collect(7).astype(jnp.bfloat16), "tensor").astype(jnp.float32),
    )
    mod_low = mod_sum.astype(jnp.bfloat16)
    ada_w_grad = (
        silu_cond.astype(jnp.float32)[None, :, None] * mod_low.astype(jnp.float32)[:, None, :]
    )
    ada_b_grad = mod_low.astype(jnp.float32)
    silu_grad = jnp.einsum("lm,ldm->d", mod_low, ada_weight, preferred_element_type=jnp.float32)
    cond_grad = silu_back(silu_grad)[0]
    summed = (
        lax.psum(ada_w_grad.astype(jnp.bfloat16), "dp").astype(jnp.float32),
        lax.psum(ada_b_grad.astype(jnp.bfloat16), "dp").astype(jnp.float32),
        lax.psum(collect(0).astype(jnp.bfloat16), "dp").astype(jnp.float32),
        lax.psum(collect(1).astype(jnp.bfloat16), "dp").astype(jnp.float32),
        lax.psum(collect(2).astype(jnp.bfloat16), "dp").astype(jnp.float32),
        lax.psum(out_b_sum.astype(jnp.bfloat16), "dp").astype(jnp.float32),
        lax.psum(collect(4).astype(jnp.bfloat16), "dp").astype(jnp.float32),
        lax.psum(collect(5).astype(jnp.bfloat16), "dp").astype(jnp.float32),
        lax.psum(collect(6).astype(jnp.bfloat16), "dp").astype(jnp.float32),
        lax.psum(fc2_b_sum.astype(jnp.bfloat16), "dp").astype(jnp.float32),
    )
    return (
        layer_output,
        stream_grad.astype(jnp.bfloat16)[None],
        cond_grad.astype(jnp.bfloat16)[None],
        summed[0],
        summed[1],
        summed[2],
        summed[3],
        summed[4],
        summed[5],
        summed[6],
        summed[7],
        summed[8],
        summed[9],
    )


def solution(mesh):
    in_specs = (
        P("dp", "tensor", None),
        P("dp", "tensor"),
        P(None, "tensor", None),
        P(),
        P(None, None, None, "tensor"),
        P(None, None, "tensor"),
        P(None, "tensor", None),
        P(),
        P(None, None, "tensor"),
        P(None, "tensor"),
        P(None, "tensor", None),
        P(),
        P("dp", "tensor", None),
    )
    out_specs = (
        P("dp", "tensor", None),
        P("dp", "tensor", None),
        P("dp", "tensor"),
        P(None, "tensor", None),
        P(),
        P(None, None, None, "tensor"),
        P(None, None, "tensor"),
        P(None, "tensor", None),
        P(),
        P(None, None, "tensor"),
        P(None, "tensor"),
        P(None, "tensor", None),
        P(),
    )
    return jax.shard_map(
        per_device, mesh=mesh, in_specs=in_specs, out_specs=out_specs, check_vma=False
    )
```

profile of v0, /device:TPU:0, one launch (start us, length us, event | category | flops | bytes accessed | tf_op | source)
XLA Modules:
  0.0 1360.1 jit_solution(16830422912774858308)
XLA Ops:
  11.1 2.8 fusion.180
  14.0 30.9 %psum.98 = f32[2,6912]{1,0:T(2,128)S(1)} all-reduce(f32[2,6912]{1,0:T(2,128)S(1)} %bitcast.362), channel_id=1, replica_groups=mesh['dp'=4,'tensor'=8] {'tensor'}, use_global_device_ids=true, to_apply=%region_0.1 | all-reduce | flops 13824 | bytes 110592 | tf_op jit(solution)/shard_map/psum | solution.py:263
  48.3 48.6 %all-gather.9.cloned.1.call-done = bf16[2048,1152]{1,0:T(8,128)(2,1)} async-done(((bf16[256,1152]{1,0:T(8,128)(2,1)}), bf16[2048,1152]{1,0:T(8,128)(2,1)}) %all-gather.9.cloned.1.call-update) | async-done | bytes 4718608 | tf_op jit(solution)/shard_map/all_gather | solution.py:90
  96.8 5.1 fusion.181
  104.4 3.2 fusion.168
  110.7 3.8 convolution_convert_fusion.7
  115.8 52.6 %reduce-scatter.9.cloned.1.call-done = bf16[256,1152]{1,0:T(8,128)(2,1)} async-done(((bf16[2048,1152]{1,0:T(8,128)(2,1)}), bf16[256,1152]{1,0:T(8,128)(2,1)}) %reduce-scatter.9.cloned.1.call-update) | async-done | bytes 589840 | tf_op jit(solution)/shard_map/reduce_scatter | solution.py:94
  173.6 49.3 %all-gather.11.cloned.1.call-done = bf16[2048,1152]{1,0:T(8,128)(2,1)} async-done(((bf16[256,1152]{1,0:T(8,128)(2,1)}), bf16[2048,1152]{1,0:T(8,128)(2,1)}) %all-gather.11.cloned.1.call-update) | async-done | bytes 4718608 | tf_op jit(solution)/shard_map/all_gather | solution.py:90
  223.0 5.6 fusion.59
  228.7 2.2 copy-done.121
  230.9 6.7 convolution_convert_fusion.6
  238.9 52.6 %reduce-scatter.11.cloned.1.call-done = bf16[256,1152]{1,0:T(8,128)(2,1)} async-done(((bf16[2048,1152]{1,0:T(8,128)(2,1)}), bf16[256,1152]{1,0:T(8,128)(2,1)}) %reduce-scatter.11.cloned.1.call-update) | async-done | bytes 589840 | tf_op jit(solution)/shard_map/reduce_scatter | solution.py:94
  294.5 50.2 %all-gather.13.cloned.1.call-done = bf16[2048,1152]{1,0:T(8,128)(2,1)} async-done(((bf16[256,1152]{1,0:T(8,128)(2,1)}), bf16[2048,1152]{1,0:T(8,128)(2,1)}) %all-gather.13.cloned.1.call-update) | async-done | bytes 4718608 | tf_op jit(solution)/shard_map/all_gather | solution.py:90
  344.7 4.8 fusion.182
  356.7 5.3 fusion.169
  362.0 3.7 fusion.40
  368.6 4.8 convolution_convert_fusion.5
  373.4 53.9 %reduce-scatter.13.cloned.1.call-done = bf16[256,1152]{1,0:T(8,128)(2,1)} async-done(((bf16[2048,1152]{1,0:T(8,128)(2,1)}), bf16[256,1152]{1,0:T(8,128)(2,1)}) %reduce-scatter.13.cloned.1.call-update) | async-done | bytes 589840 | tf_op jit(solution)/shard_map/reduce_scatter | solution.py:94
  431.9 2.6 fusion.159
  435.0 47.1 %all-gather.15.cloned.1.call-done = bf16[2048,1152]{1,0:T(8,128)(2,1)} async-done(((bf16[256,1152]{1,0:T(8,128)(2,1)}), bf16[2048,1152]{1,0:T(8,128)(2,1)}) %all-gather.15.cloned.1.call-update) | async-done | bytes 4718608 | tf_op jit(solution)/shard_map/all_gather | solution.py:90
  482.1 8.2 fusion.51
  490.2 44.6 %all-gather.17.cloned.1.call-done = bf16[2048,1152]{1,0:T(8,128)(2,1)} async-done(((bf16[256,1152]{1,0:T(8,128)(2,1)}), bf16[2048,1152]{1,0:T(8,128)(2,1)}) %all-gather.17.cloned.1.call-update) | async-done | bytes 4718608 | tf_op jit(solution)/shard_map/all_gather | solution.py:100
  534.8 9.9 fusion.178
  546.2 5.8 convolution_convert_fusion.3
  552.2 10.0 convolution_convert_fusion.4
  562.3 43.6 %reduce-scatter.17.cloned.1.call-done = bf16[256,1152]{1,0:T(8,128)(2,1)} async-done(((bf16[2048,1152]{1,0:T(8,128)(2,1)}), bf16[256,1152]{1,0:T(8,128)(2,1)}) %reduce-scatter.17.cloned.1.call-update) | async-done | bytes 589840 | tf_op jit(solution)/shard_map/reduce_scatter | solution.py:104
  605.9 2.1 fusion.74
  609.3 52.7 %reduce-scatter.15.cloned.1.call-done = bf16[256,1152]{1,0:T(8,128)(2,1)} async-done(((bf16[2048,1152]{1,0:T(8,128)(2,1)}), bf16[256,1152]{1,0:T(8,128)(2,1)}) %reduce-scatter.15.cloned.1.call-update) | async-done | bytes 589840 | tf_op jit(solution)/shard_map/reduce_scatter | solution.py:94
  662.0 2.7 fusion.164
  667.7 50.0 %all-gather.19.cloned.1.call-done = bf16[2048,1152]{1,0:T(8,128)(2,1)} async-done(((bf16[256,1152]{1,0:T(8,128)(2,1)}), bf16[2048,1152]{1,0:T(8,128)(2,1)}) %all-gather.19.cloned.1.call-update) | async-done | bytes 4718608 | tf_op jit(solution)/shard_map/all_gather | solution.py:100
  717.7 4.0 convolution_convert_fusion.17
  723.7 4.3 fusion.174
  731.7 2.3 fusion.175
  744.6 4.6 convolution_convert_fusion.1
  749.3 53.9 %reduce-scatter.19.cloned.1.call-done = bf16[256,1152]{1,0:T(8,128)(2,1)} async-done(((bf16[2048,1152]{1,0:T(8,128)(2,1)}), bf16[256,1152]{1,0:T(8,128)(2,1)}) %reduce-scatter.19.cloned.1.call-update) | async-done | bytes 589840 | tf_op jit(solution)/shard_map/reduce_scatter | solution.py:104
  805.2 2.2 fusion.75
  807.6 2.5 fusion.158
  810.4 49.9 %all-gather.21.cloned.1.call-done = bf16[2048,1152]{1,0:T(8,128)(2,1)} async-done(((bf16[256,1152]{1,0:T(8,128)(2,1)}), bf16[2048,1152]{1,0:T(8,128)(2,1)}) %all-gather.21.cloned.1.call-update) | async-done | bytes 4718608 | tf_op jit(solution)/shard_map/all_gather | solution.py:100
  860.3 9.9 fusion.179
  871.6 5.8 convolution_convert_fusion.2
  877.5 53.9 %reduce-scatter.21.cloned.1.call-done = bf16[256,1152]{1,0:T(8,128)(2,1)} async-done(((bf16[2048,1152]{1,0:T(8,128)(2,1)}), bf16[256,1152]{1,0:T(8,128)(2,1)}) %reduce-scatter.21.cloned.1.call-update) | async-done | bytes 589840 | tf_op jit(solution)/shard_map/reduce_scatter | solution.py:104
  931.4 2.4 fusion.76
  937.0 49.7 %all-gather.23.cloned.1.call-done = bf16[2048,1152]{1,0:T(8,128)(2,1)} async-done(((bf16[256,1152]{1,0:T(8,128)(2,1)}), bf16[2048,1152]{1,0:T(8,128)(2,1)}) %all-gather.23.cloned.1.call-update) | async-done | bytes 4718608 | tf_op jit(solution)/shard_map/all_gather | solution.py:100
  986.8 4.1 convolution_convert_fusion.16
  999.2 4.6 convolution_convert_fusion
  1005.0 7.3 fusion.22
  1012.4 9.2 fusion.20
  1024.0 2.6 fusion.79
  1026.6 3.5 fusion.24
  1030.2 5.9 convolution_convert_fusion.12
  1038.2 6.4 fusion.21
  1046.4 8.2 fusion.19
  1056.7 3.5 fusion.23
  1061.1 4.9 convolution_convert_fusion.13
  1074.2 26.9 %all-reduce = (bf16[2,6912]{1,0:T(2,128)(2,1)S(1)}, bf16[2,1152]{1,0:T(2,128)(2,1)S(1)}, bf16[2,1152]{1,0:T(2,128)(2,1)S(1)}) all-reduce(bf16[2,6912]{1,0:T(2,128)(2,1)S(1)} %pad_maximum_fusion.4, bf16[2,1152]{1,0:T(2,128)(2,1)S(1)} %get-tuple-element.108, ...), channel_id=1, replica_groups=mesh['dp'=4,'tensor'=8] {'tensor'}, use_global_device_ids=true, to_apply=%region_43.44 | all-reduce | flops 18432 | bytes 73728 | tf_op jit(solution)/shard_map/psum | solution.py:298
  1101.1 2.5 multiply_convert_fusion
  1104.6 3.2 fusion.128
  1108.5 18.3 %all-reduce.1 = (bf16[2,6912]{1,0:T(2,128)(2,1)S(1)}, bf16[2,2,144]{2,1,0:T(2,128)(2,1)S(1)}, bf16[2,1152]{1,0:T(2,128)(2,1)S(1)}, bf16[2,576]{1,0:T(2,128)(2,1)S(1)}, bf16[2,1152]{1,0:T(2,128)(2,1)S(1)}) all-reduce(bf16[2,6912]{1,0:T(2,128)(2,1)S(1)} %get-tuple-element.41, ...), channel_id=1, replica_groups=mesh['dp'=4,'tensor'=8] {'dp'}, use_global_device_ids=true, to_apply=%region_45.46 | all-reduce | flops 20160 | bytes 80640 | tf_op jit(solution)/shard_map/psum | solution.py:311
  1129.9 206.3 %all-reduce.5.cloned.1.call-done = (bf16[2,144,6912]{2,1,0:T(8,128)(2,1)}, bf16[2,1152,3,144]{1,3,2,0:T(8,128)(2,1)}, bf16[2,144,1152]{2,1,0:T(8,128)(2,1)}, bf1...) async-done(((bf16[2,144,6912]{2,1,0:T(8,128)(2,1)}, bf16[2,1152,3,144]{1,3,2,0:T(8,128)(2,1)}, bf16[2,144,1152]{2,1,0:T(8,128)(2,1)}, bf16[2,1152,576]{1,2,0:T(8,128)(2,1)}, ...) | async-done | bytes 11943952 | tf_op jit(solution)/shard_map/psum | solution.py:310
  1336.2 2.2 convert_element_type.435
  1338.4 6.0 convert_element_type.427
  1344.5 2.2 convert_element_type.429
  1347.5 2.7 convert_element_type.439
  1350.4 2.7 convert_element_type.443
  (423 shorter events, 100.0 us)
Async XLA Ops:
  7.2 89.7 %all-gather.9.cloned.1.call-start = ((), (), s32[]{:S(2)}) async-start(), calls=%async_computation.8 | async-start | bytes 5308416 | tf_op jit(solution)/shard_map/all_gather | solution.py:90
  7.9 6.0 copy-start.105
  9.1 36.5 %copy-start.66 = (f32[256]{0:T(256)}, f32[256]{0:T(256)S(1)}, u32[]{:S(2)}) copy-start(f32[256]{0:T(256)S(1)} %broadcast_multiply_fusion.3) | copy-start | bytes 3076
  10.5 35.1 %copy-start.78 = (f32[256]{0:T(256)}, f32[256]{0:T(256)S(1)}, u32[]{:S(2)}) copy-start(f32[256]{0:T(256)S(1)} %fusion.137) | copy-start | bytes 3076
  11.1 33.7 %copy-start.68 = (bf16[2,6912]{1,0:T(2,128)(2,1)S(1)}, bf16[2,6912]{1,0:T(2,128)(2,1)}, u32[]{:S(2)}) copy-start(bf16[2,6912]{1,0:T(2,128)(2,1)} %param.16) | copy-start | bytes 82948
  11.1 34.5 %copy-start = (bf16[1,256,1152]{2,1,0:T(8,128)(2,1)S(1)}, bf16[1,256,1152]{2,1,0:T(8,128)(2,1)}, u32[]{:S(2)}) copy-start(bf16[1,256,1152]{2,1,0:T(8,128)(2,1)} %param.13) | copy-start | bytes 1769476
  13.9 32.9 %copy-start.107 = (bf16[2,2,144]{2,1,0:T(2,128)(2,1)S(1)}, bf16[2,2,144]{2,1,0:T(2,128)(2,1)}, u32[]{:S(2)}) copy-start(bf16[2,2,144]{2,1,0:T(2,128)(2,1)} %param.18) | copy-start | bytes 3460
  13.9 32.9 %copy-start.30 = (bf16[2,1152,3,144]{1,3,2,0:T(8,128)(2,1)S(1)}, bf16[2,1152,3,144]{1,3,2,0:T(8,128)(2,1)}, u32[]{:S(2)}) copy-start(bf16[2,1152,3,144]{1,3,2,0:T(8,128)(2,1)} %param.17) | copy-start | bytes 5971972
  45.6 125.8 %copy-start.54 = (f32[1152]{0:T(1024)}, f32[1152]{0:T(1024)S(1)}, u32[]{:S(2)}) copy-start(f32[1152]{0:T(1024)S(1)} %get-tuple-element.30) | copy-start | bytes 13828
  45.6 245.9 %copy-start.59 = (f32[1152]{0:T(1024)}, f32[1152]{0:T(1024)S(1)}, u32[]{:S(2)}) copy-start(f32[1152]{0:T(1024)S(1)} %get-tuple-element.31) | copy-start | bytes 13828
  45.6 247.8 %copy-start.48 = (f32[1152]{0:T(1024)}, f32[1152]{0:T(1024)S(1)}, u32[]{:S(2)}) copy-start(f32[1152]{0:T(1024)S(1)} %get-tuple-element.27) | copy-start | bytes 13828
  46.8 121.7 %reduce-scatter.9.cloned.1.call-start = ((), (), s32[]{:S(2)}) async-start(), calls=%async_computation.9 | async-start | bytes 5308416 | tf_op jit(solution)/shard_map/reduce_scatter | solution.py:94
  114.6 108.4 %all-gather.11.cloned.1.call-start = ((), (), s32[]{:S(2)}) async-start(), calls=%async_computation.10 | async-start | bytes 5308416 | tf_op jit(solution)/shard_map/all_gather | solution.py:90
  169.9 58.7 %copy-start.69 = (f32[256]{0:T(256)}, f32[256]{0:T(256)S(1)}, u32[]{:S(2)}) copy-start(f32[256]{0:T(256)S(1)} %broadcast_multiply_fusion.2) | copy-start | bytes 3076
  171.4 57.2 %copy-start.101 = (f32[256]{0:T(256)}, f32[256]{0:T(256)S(1)}, u32[]{:S(2)}) copy-start(f32[256]{0:T(256)S(1)} %multiply_reduce_fusion.9) | copy-start | bytes 3076
  171.4 57.2 %copy-start.80 = (f32[256]{0:T(256)}, f32[256]{0:T(256)S(1)}, u32[]{:S(2)}) copy-start(f32[256]{0:T(256)S(1)} %fusion.138) | copy-start | bytes 3076
  172.7 118.8 %reduce-scatter.11.cloned.1.call-start = ((), (), s32[]{:S(2)}) async-start(), calls=%async_computation.11 | async-start | bytes 5308416 | tf_op jit(solution)/shard_map/reduce_scatter | solution.py:94
  173.6 55.0 %copy-start.109 = (f32[576]{0:T(1024)}, f32[576]{0:T(1024)S(1)}, u32[]{:S(2)}) copy-start(f32[576]{0:T(1024)S(1)} %get-tuple-element.40) | copy-start | bytes 6916
  223.0 7.9 copy-start.116
  237.6 107.1 %all-gather.13.cloned.1.call-start = ((), (), s32[]{:S(2)}) async-start(), calls=%async_computation.12 | async-start | bytes 5308416 | tf_op jit(solution)/shard_map/all_gather | solution.py:90
  238.9 55.6 %copy-start.57 = (f32[1152]{0:T(1024)}, f32[1152]{0:T(1024)S(1)}, u32[]{:S(2)}) copy-start(f32[1152]{0:T(1024)S(1)} %get-tuple-element.36) | copy-start | bytes 13828
  293.0 51.7 %copy-start.37 = (bf16[1,1152,3,144]{1,3,2,0:T(8,128)(2,1)S(1)}, bf16[1,1152,3,144]{1,3,2,0:T(8,128)(2,1)}, u32[]{:S(2)}) copy-start(bf16[1,1152,3,144]{1,3,2,0:T(8,128)(2,1)} %get-tuple-element.78) | copy-start | bytes 2985988
  293.1 56.5 %copy-start.64 = (f32[256]{0:T(256)}, f32[256]{0:T(256)S(1)}, u32[]{:S(2)}) copy-start(f32[256]{0:T(256)S(1)} %broadcast_multiply_fusion.1) | copy-start | bytes 3076
  293.3 56.2 %copy-start.103 = (f32[256]{0:T(256)}, f32[256]{0:T(256)S(1)}, u32[]{:S(2)}) copy-start(f32[256]{0:T(256)S(1)} %multiply_reduce_fusion.8) | copy-start | bytes 3076
  293.4 56.2 %copy-start.76 = (f32[256]{0:T(256)}, f32[256]{0:T(256)S(1)}, u32[]{:S(2)}) copy-start(f32[256]{0:T(256)S(1)} %fusion.139) | copy-start | bytes 3076
  294.5 132.8 %reduce-scatter.13.cloned.1.call-start = ((), (), s32[]{:S(2)}) async-start(), calls=%async_computation.13 | async-start | bytes 5308416 | tf_op jit(solution)/shard_map/reduce_scatter | solution.py:94
  373.4 108.7 %all-gather.15.cloned.1.call-start = ((), (), s32[]{:S(2)}) async-start(), calls=%async_computation.14 | async-start | bytes 5308416 | tf_op jit(solution)/shard_map/all_gather | solution.py:90
  431.9 103.0 %all-gather.17.cloned.1.call-start = ((), (), s32[]{:S(2)}) async-start(), calls=%async_computation.16 | async-start | bytes 5308416 | tf_op jit(solution)/shard_map/all_gather | solution.py:100
  434.5 171.4 %reduce-scatter.17.cloned.1.call-start = ((), (), s32[]{:S(2)}) async-start(), calls=%async_computation.17 | async-start | bytes 5308416 | tf_op jit(solution)/shard_map/reduce_scatter | solution.py:104
  534.8 11.3 copy-start.117
  552.0 110.0 %reduce-scatter.15.cloned.1.call-start = ((), (), s32[]{:S(2)}) async-start(), calls=%async_computation.15 | async-start | bytes 5308416 | tf_op jit(solution)/shard_map/reduce_scatter | solution.py:94
  562.3 155.4 %all-gather.19.cloned.1.call-start = ((), (), s32[]{:S(2)}) async-start(), calls=%async_computation.18 | async-start | bytes 5308416 | tf_op jit(solution)/shard_map/all_gather | solution.py:100
  664.7 53.0 %copy-start.41 = (bf16[2,144,1152]{2,1,0:T(8,128)(2,1)S(1)}, bf16[2,144,1152]{2,1,0:T(8,128)(2,1)}, u32[]{:S(2)}) copy-start(bf16[2,144,1152]{2,1,0:T(8,128)(2,1)} %param.19) | copy-start | bytes 1990660
  664.7 53.0 %copy-start.82 = (f32[256]{0:T(256)}, f32[256]{0:T(256)S(1)}, u32[]{:S(2)}) copy-start(f32[256]{0:T(256)S(1)} %negate_multiply_fusion.3) | copy-start | bytes 3076
  667.5 135.6 %reduce-scatter.19.cloned.1.call-start = ((), (), s32[]{:S(2)}) async-start(), calls=%async_computation.19 | async-start | bytes 5308416 | tf_op jit(solution)/shard_map/reduce_scatter | solution.py:104
  749.2 58.3 %copy-start.3 = (f32[256,1152]{1,0:T(8,128)S(1)}, f32[256,1152]{1,0:T(8,128)}, u32[]{:S(2)}) copy-start(f32[256,1152]{1,0:T(8,128)} %copy-done.2) | copy-start | bytes 3538948
  749.2 111.1 %all-gather.21.cloned.1.call-start = ((), (), s32[]{:S(2)}) async-start(), calls=%async_computation.20 | async-start | bytes 5308416 | tf_op jit(solution)/shard_map/all_gather | solution.py:100
  810.1 121.3 %reduce-scatter.21.cloned.1.call-start = ((), (), s32[]{:S(2)}) async-start(), calls=%async_computation.21 | async-start | bytes 5308416 | tf_op jit(solution)/shard_map/reduce_scatter | solution.py:104
  860.3 11.3 copy-start.118
  877.4 54.0 %copy-start.55 = (f32[1152]{0:T(1024)S(1)}, f32[1152]{0:T(1024)}, u32[]{:S(2)}) copy-start(f32[1152]{0:T(1024)} %copy-done.54) | copy-start | bytes 13828
  877.4 54.0 %copy-start.70 = (f32[256]{0:T(256)S(1)}, f32[256]{0:T(256)}, u32[]{:S(2)}) copy-start(f32[256]{0:T(256)} %copy-done.69) | copy-start | bytes 3076
  877.4 54.0 %copy-start.81 = (f32[256]{0:T(256)S(1)}, f32[256]{0:T(256)}, u32[]{:S(2)}) copy-start(f32[256]{0:T(256)} %copy-done.80) | copy-start | bytes 3076
  877.4 56.3 %copy-start.102 = (f32[256]{0:T(256)S(1)}, f32[256]{0:T(256)}, u32[]{:S(2)}) copy-start(f32[256]{0:T(256)} %copy-done.101) | copy-start | bytes 3076
  877.5 56.9 %copy-start.7 = (f32[256,1152]{1,0:T(8,128)S(1)}, f32[256,1152]{1,0:T(8,128)}, u32[]{:S(2)}) copy-start(f32[256,1152]{1,0:T(8,128)} %get-tuple-element.58) | copy-start | bytes 3538948
  877.5 109.3 %all-gather.23.cloned.1.call-start = ((), (), s32[]{:S(2)}) async-start(), calls=%async_computation.22 | async-start | bytes 5308416 | tf_op jit(solution)/shard_map/all_gather | solution.py:100
  934.4 52.4 %copy-start.42 = (bf16[2,144,1152]{2,1,0:T(8,128)(2,1)S(1)}, bf16[2,144,1152]{2,1,0:T(8,128)(2,1)}, u32[]{:S(2)}) copy-start(bf16[2,144,1152]{2,1,0:T(8,128)(2,1)} %param.19) | copy-start | bytes 1990660
  936.5 54.5 %copy-start.63 = (f32[8,2,256]{2,1,0:T(2,128)S(1)}, f32[8,2,256]{2,1,0:T(2,128)}, u32[]{:S(2)}) copy-start(f32[8,2,256]{2,1,0:T(2,128)} %copy-done.62) | copy-start | bytes 49156
  936.5 130.9 %reduce-scatter.23.cloned.1.call-start = ((), (), s32[]{:S(2)}) async-start(), calls=%async_computation.23 | async-start | bytes 5308416 | tf_op jit(solution)/shard_map/reduce_scatter | solution.py:104
  1003.8 332.4 %all-reduce.5.cloned.1.call-start = ((), (), s32[]{:S(2)}) async-start(), calls=%async_computation.24 | async-start | bytes 23887872 | tf_op jit(solution)/shard_map/psum | solution.py:310
  1005.0 7.3 copy-start.111
  1012.4 9.2 copy-start.93
  1012.4 11.6 copy-start.4
  1012.4 11.6 copy-start.56
  1030.1 6.3 copy-start.87
  1030.1 6.5 copy-start.91
  1030.1 6.8 copy-start.90
  1030.1 7.1 copy-start.85
  1030.2 7.3 copy-start.89
  1030.2 7.8 copy-start.28
  1030.2 7.8 copy-start.58
  1038.2 6.5 copy-start.33
  1046.4 8.2 copy-start.32
  1070.9 30.2 %copy-start.108 = (f32[144]{0:T(256)S(1)}, f32[144]{0:T(256)}, u32[]{:S(2)}) copy-start(f32[144]{0:T(256)} %get-tuple-element.54) | copy-start | bytes 1732
  1338.4 6.0 copy-start.31
  (77 other events, 201.4 us)
Sparse Core Ops, SparseCore 0:
  46.9 49.9 all-gather.8
  114.7 53.7 reduce-scatter.8
  172.9 50.0 all-gather.10
  237.7 53.7 reduce-scatter.10
  294.6 50.0 all-gather.12
  373.5 53.7 reduce-scatter.12
  432.0 50.0 all-gather.14
  484.3 50.5 all-gather.16
  552.1 53.7 reduce-scatter.16
  608.7 53.3 reduce-scatter.14
  667.6 50.0 all-gather.18
  749.3 53.7 reduce-scatter.18
  810.2 50.0 all-gather.20
  877.6 53.7 reduce-scatter.20
  936.6 50.0 all-gather.22
  1003.9 53.7 reduce-scatter.22
  1103.7 232.4 all-reduce.4
where the time goes:
time: 1370 us; the launch traced here: 1360 us
  waiting for transfers between devices  959 us (70%)
  matrix products  176 us (13%)
  other arithmetic  82.1 us (6%)
  blocking collectives  76 us (6%)
  local copies, waits for them, and re-layouts  48.3 us (4%)
  between operations  16 us (1%)
    reduce_scatter x4, waiting for transfers between devices, reduce_rows(): lax.psum_scatter(partial_terms.astype(jnp.bfloat16), 'tensor', scatter_di...  212 us
    psum x1, waiting for transfers between devices, per_device(): lax.psum(ada_w_grad.astype(jnp.bfloat16), 'dp').astype(jnp.float32)  206 us
    all_gather x4, waiting for transfers between devices, spread_rows(): return lax.all_gather(row_block, 'tensor', axis=0, tiled=True)  195 us
    all_gather x4, waiting for transfers between devices, spread_grads(): return lax.all_gather(row_block, 'tensor', axis=0, tiled=True)  194 us
    reduce_scatter x4, waiting for transfers between devices, reduce_grads(): lax.psum_scatter(partial_terms.astype(jnp.bfloat16), 'tensor', scatter_di...  151 us
    psum x1, blocking collectives, per_device(): modulations = lax.psum(ada_terms, 'tensor') + ada_bias.astype(jnp.float32)  30.9 us
    unnamed x278, local copies, waits for them, and re-layouts  27.9 us
  transfers between devices with their start and end apart: 17, of which 16 were waited for; matrix products, arithmetic and copies ran while one was open for 7% of the time, Pallas kernels for 0%

commit v1 on v0

--- a/solution.py
+++ b/solution.py
@@ -1,3 +1,4 @@
+import functools
 from functools import partial
 import jax
 import jax.numpy as jnp
@@ -8,6 +9,31 @@
 PATCHES = 256
 FRAMES = 8
 LAYERS = 2
+
+
+def resolve_chains_for(block_in, array_axis):
+    odd = list(block_in.shape[1:])
+    odd[array_axis] *= block_in.shape[0]
+    return jnp.moveaxis(block_in, 0, array_axis).reshape(odd)
+
+
+def turn_run(shard_in, which_axis, array_dim):
+    dev_count = lax.axis_size(which_axis)
+    series = [(src_i, (src_i + 1) % dev_count) for src_i in range(dev_count)]
+    bank = [(idx, h) for h, idx in series]
+    high, then = ([], [])
+    for p in range(dev_count - 1):
+        if p % 2 == 0:
+            high.append(lax.ppermute(high[-1] if high else shard_in, which_axis, series))
+        else:
+            then.append(lax.ppermute(then[-1] if then else shard_in, which_axis, bank))
+    s_next = jnp.stack([*high[::-1], shard_in, *then])
+    outer = lax.axis_index(which_axis) - len(high)
+    s_next = s_next[(jnp.arange(dev_count) - outer) % dev_count]
+    return resolve_chains_for(s_next, array_dim)
+
+
+choose_the_quarters = functools.partial(turn_run, which_axis="tensor", array_dim=0)
 
 
 def normalize(stream):
@@ -87,7 +113,7 @@
 
 
 def spread_rows(row_block):
-    return lax.all_gather(row_block, "tensor", axis=0, tiled=True)
+    return choose_the_quarters(row_block)
 
 
 def reduce_rows(partial_terms):

time: 1370 us -> 1430 us (1.044)
  starting transfers between devices: 2.6 us -> 57.5 us
  local copies, waits for them, and re-layouts: 48.3 us -> 99.4 us
  waiting for transfers between devices: 959 us -> 911 us
    all_gather x4 -> x0, waiting for transfers between devices: 195 us -> none  [spread_rows(): return lax.all_gather(row_block, 'tensor', axis=0, tiled=True)]
    ppermute x0 -> x28, waiting for transfers between devices: none -> 194 us  [the longest x16 177 us: turn_run(): lax.ppermute(high[-1] if high else shard_in, which_axis, series)]
    ppermute x0 -> x28, starting transfers between devices: none -> 55.9 us  [the longest x12 55.7 us: turn_run(): then.append(lax.ppermute(then[-1] if then else shard_in, which_axis, bank))]
    all_gather x4, waiting for transfers between devices: 194 us -> 150 us  [spread_grads(): return lax.all_gather(row_block, 'tensor', axis=0, tiled=True)]
    unnamed x278 -> x315, local copies, waits for them, and re-layouts: 27.9 us -> 53 us
    gather x0 -> x4, local copies, waits for them, and re-layouts: none -> 22.6 us  [turn_run(): s_next = s_next[(jnp.arange(dev_count) - outer) % dev_count]]
  transfers between devices with their start and end apart: 17 -> 41, of which waited for: 16 -> 34; matrix products, arithmetic and copies ran while one was open for 7% -> 9% of each run, Pallas kernels for 0% -> 0%
where the time goes in v1:
time: 1430 us; the launch traced here: 1420 us
  waiting for transfers between devices  911 us (64%)
  matrix products  176 us (12%)
  local copies, waits for them, and re-layouts  99.4 us (7%)
  other arithmetic  82 us (6%)
  blocking collectives  75.9 us (5%)
  starting transfers between devices  57.5 us (4%)
  between operations  15.7 us (1%)
    reduce_scatter x4, waiting for transfers between devices, reduce_rows(): lax.psum_scatter(partial_terms.astype(jnp.bfloat16), 'tensor', scatter_di...  207 us
    psum x1, waiting for transfers between devices, per_device(): lax.psum(ada_w_grad.astype(jnp.bfloat16), 'dp').astype(jnp.float32)  206 us
    ppermute x16, waiting for transfers between devices, turn_run(): lax.ppermute(high[-1] if high else shard_in, which_axis, series)  177 us
    reduce_scatter x4, waiting for transfers between devices, reduce_grads(): lax.psum_scatter(partial_terms.astype(jnp.bfloat16), 'tensor', scatter_di...  154 us
    all_gather x4, waiting for transfers between devices, spread_grads(): return lax.all_gather(row_block, 'tensor', axis=0, tiled=True)  150 us
    ppermute x12, starting transfers between devices, turn_run(): then.append(lax.ppermute(then[-1] if then else shard_in, which_axis, bank))  55.7 us
    unnamed x315, local copies, waits for them, and re-layouts  53 us
    psum x1, blocking collectives, per_device(): modulations = lax.psum(ada_terms, 'tensor') + ada_bias.astype(jnp.float32)  30.7 us
  transfers between devices with their start and end apart: 41, of which 34 were waited for; matrix products, arithmetic and copies ran while one was open for 9% of the time, Pallas kernels for 0%

profile of v1, /device:TPU:0, one launch (start us, length us, event | category | flops | bytes accessed | tf_op | source)
XLA Modules:
  0.0 1417.2 jit_solution(10159458523506002125)
XLA Ops:
  14.1 30.7 %psum.98 = f32[2,6912]{1,0:T(2,128)S(1)} all-reduce(f32[2,6912]{1,0:T(2,128)S(1)} %bitcast.448), channel_id=1, replica_groups=mesh['dp'=4,'tensor'=8] {'tensor'}, use_global_device_ids=true, to_apply=%region_0.1 | all-reduce | flops 13824 | bytes 110592 | tf_op jit(solution)/shard_map/psum | solution.py:289
  46.7 11.5 collective-permute-done
  61.7 10.8 collective-permute-done.1
  78.3 8.5 collective-permute-done.2
  95.4 6.5 collective-permute-done.3
  112.3 5.7 gather_fusion
  117.9 4.8 fusion.190
  131.5 3.8 convolution_convert_fusion.7
  136.6 52.0 %reduce-scatter.9.cloned.1.call-done = bf16[256,1152]{1,0:T(8,128)(2,1)} async-done(((bf16[2048,1152]{1,0:T(8,128)(2,1)}), bf16[256,1152]{1,0:T(8,128)(2,1)}) %reduce-scatter.9.cloned.1.call-update) | async-done | bytes 589840 | tf_op jit(solution)/shard_map/reduce_scatter | solution.py:120
  192.1 11.1 collective-permute-done.7
  206.8 11.5 collective-permute-done.8
  218.8 3.7 collective-permute-start.12
  222.6 9.6 collective-permute-done.9
  236.1 4.1 collective-permute-start.13
  240.2 6.5 collective-permute-done.10
  253.7 5.6 gather_fusion.1
  259.3 5.6 fusion.61
  267.1 6.7 convolution_convert_fusion.6
  275.1 51.9 %reduce-scatter.11.cloned.1.call-done = bf16[256,1152]{1,0:T(8,128)(2,1)} async-done(((bf16[2048,1152]{1,0:T(8,128)(2,1)}), bf16[256,1152]{1,0:T(8,128)(2,1)}) %reduce-scatter.11.cloned.1.call-update) | async-done | bytes 589840 | tf_op jit(solution)/shard_map/reduce_scatter | solution.py:120
  329.2 11.1 collective-permute-done.14
  343.9 11.5 collective-permute-done.15
  359.7 9.6 collective-permute-done.16
  369.2 4.0 collective-permute-done.19
  373.2 3.8 collective-permute-start.20
  377.0 5.9 collective-permute-done.17
  390.1 5.7 gather_fusion.2
  395.8 4.8 fusion.191
  407.7 5.4 fusion.178
  419.8 4.8 convolution_convert_fusion.5
  427.2 50.6 %reduce-scatter.13.cloned.1.call-done = bf16[256,1152]{1,0:T(8,128)(2,1)} async-done(((bf16[2048,1152]{1,0:T(8,128)(2,1)}), bf16[256,1152]{1,0:T(8,128)(2,1)}) %reduce-scatter.13.cloned.1.call-update) | async-done | bytes 589840 | tf_op jit(solution)/shard_map/reduce_scatter | solution.py:120
  481.1 14.3 %collective-permute-done.21 = bf16[256,1152]{1,0:T(8,128)(2,1)S(1)} collective-permute-done((bf16[256,1152]{1,0:T(8,128)(2,1)S(1)}, bf16[256,1152]{1,0:T(8,128)(2,1)S(1)}, u32[]{:S(2)}, u32[]{:S(2)}) %collective-permute-start.21) | collective-permute-done | bytes 589856 | tf_op jit(solution)/shard_map/ppermute | solution.py:27
  498.9 25.3 %collective-permute-done.22 = bf16[256,1152]{1,0:T(8,128)(2,1)S(1)} collective-permute-done((bf16[256,1152]{1,0:T(8,128)(2,1)S(1)}, bf16[256,1152]{1,0:T(8,128)(2,1)S(1)}, u32[]{:S(2)}, u32[]{:S(2)}) %collective-permute-start.22) | collective-permute-done | bytes 589856 | tf_op jit(solution)/shard_map/ppermute | solution.py:27
  524.2 3.7 collective-permute-start.26
  528.0 22.9 %collective-permute-done.23 = bf16[256,1152]{1,0:T(8,128)(2,1)S(1)} collective-permute-done((bf16[256,1152]{1,0:T(8,128)(2,1)S(1)}, bf16[256,1152]{1,0:T(8,128)(2,1)S(1)}, u32[]{:S(2)}, u32[]{:S(2)}) %collective-permute-start.23) | collective-permute-done | bytes 589856 | tf_op jit(solution)/shard_map/ppermute | solution.py:27
  553.0 15.1 %collective-permute-start.27 = (bf16[256,1152]{1,0:T(8,128)(2,1)S(1)}, bf16[256,1152]{1,0:T(8,128)(2,1)S(1)}, u32[]{:S(2)}, u32[]{:S(2)}) collective-permute-start(bf16[256,1152]{1,0:T(8,128)(2,1)S(1)} %collective-permute-done.26), channel_id=1, source_target_pairs={{1,0},{2,1},{3,2},{4,3},{5,4},{6,5},{7,6},{0,7},{9,8},{10,9},{11,1... | collective-permute-start | bytes 1769480 | tf_op jit(solution)/shard_map/ppermute | solution.py:29
  576.4 5.6 gather_fusion.3
  582.0 8.2 fusion.53
  590.2 9.9 fusion.187
  601.5 5.8 convolution_convert_fusion.3
  607.4 10.0 convolution_convert_fusion.4
  617.5 46.3 %reduce-scatter.17.cloned.1.call-done = bf16[256,1152]{1,0:T(8,128)(2,1)} async-done(((bf16[2048,1152]{1,0:T(8,128)(2,1)}), bf16[256,1152]{1,0:T(8,128)(2,1)}) %reduce-scatter.17.cloned.1.call-update) | async-done | bytes 589840 | tf_op jit(solution)/shard_map/reduce_scatter | solution.py:130
  667.2 52.1 %reduce-scatter.15.cloned.1.call-done = bf16[256,1152]{1,0:T(8,128)(2,1)} async-done(((bf16[2048,1152]{1,0:T(8,128)(2,1)}), bf16[256,1152]{1,0:T(8,128)(2,1)}) %reduce-scatter.15.cloned.1.call-update) | async-done | bytes 589840 | tf_op jit(solution)/shard_map/reduce_scatter | solution.py:120
  725.0 50.0 %all-gather.7.cloned.1.call-done = bf16[2048,1152]{1,0:T(8,128)(2,1)} async-done(((bf16[256,1152]{1,0:T(8,128)(2,1)}), bf16[2048,1152]{1,0:T(8,128)(2,1)}) %all-gather.7.cloned.1.call-update) | async-done | bytes 4718608 | tf_op jit(solution)/shard_map/all_gather | solution.py:126
  775.0 4.0 convolution_convert_fusion.17
  780.9 4.3 fusion.183
  801.9 4.6 convolution_convert_fusion.1
  806.5 53.9 %reduce-scatter.19.cloned.1.call-done = bf16[256,1152]{1,0:T(8,128)(2,1)} async-done(((bf16[2048,1152]{1,0:T(8,128)(2,1)}), bf16[256,1152]{1,0:T(8,128)(2,1)}) %reduce-scatter.19.cloned.1.call-update) | async-done | bytes 589840 | tf_op jit(solution)/shard_map/reduce_scatter | solution.py:130
  867.8 49.8 %all-gather.9.cloned.1.call-done = bf16[2048,1152]{1,0:T(8,128)(2,1)} async-done(((bf16[256,1152]{1,0:T(8,128)(2,1)}), bf16[2048,1152]{1,0:T(8,128)(2,1)}) %all-gather.9.cloned.1.call-update) | async-done | bytes 4718608 | tf_op jit(solution)/shard_map/all_gather | solution.py:126
  917.6 9.9 fusion.188
  928.8 5.8 convolution_convert_fusion.2
  934.7 53.8 %reduce-scatter.21.cloned.1.call-done = bf16[256,1152]{1,0:T(8,128)(2,1)} async-done(((bf16[2048,1152]{1,0:T(8,128)(2,1)}), bf16[256,1152]{1,0:T(8,128)(2,1)}) %reduce-scatter.21.cloned.1.call-update) | async-done | bytes 589840 | tf_op jit(solution)/shard_map/reduce_scatter | solution.py:130
  993.9 50.0 %all-gather.11.cloned.1.call-done = bf16[2048,1152]{1,0:T(8,128)(2,1)} async-done(((bf16[256,1152]{1,0:T(8,128)(2,1)}), bf16[2048,1152]{1,0:T(8,128)(2,1)}) %all-gather.11.cloned.1.call-update) | async-done | bytes 4718608 | tf_op jit(solution)/shard_map/all_gather | solution.py:126
  1043.9 4.1 convolution_convert_fusion.16
  1056.3 4.6 convolution_convert_fusion
  1062.2 7.3 fusion.22
  1069.5 9.2 fusion.20
  1087.3 5.9 fusion.24
  1095.4 6.4 fusion.21
  1103.6 8.2 fusion.19
  1118.3 4.9 fusion.23
  1131.6 26.9 %all-reduce = (bf16[2,6912]{1,0:T(2,128)(2,1)S(1)}, bf16[2,1152]{1,0:T(2,128)(2,1)S(1)}, bf16[2,1152]{1,0:T(2,128)(2,1)S(1)}) all-reduce(bf16[2,6912]{1,0:T(2,128)(2,1)S(1)} %pad_maximum_fusion.4, bf16[2,1152]{1,0:T(2,128)(2,1)S(1)} %get-tuple-element.108, ...), channel_id=1, replica_groups=mesh['dp'=4,'tensor'=8] {'tensor'}, use_global_device_ids=true, to_apply=%region_43.44 | all-reduce | flops 18432 | bytes 73728 | tf_op jit(solution)/shard_map/psum | solution.py:324
  1166.0 18.3 %all-reduce.1 = (bf16[2,6912]{1,0:T(2,128)(2,1)S(1)}, bf16[2,2,144]{2,1,0:T(2,128)(2,1)S(1)}, bf16[2,1152]{1,0:T(2,128)(2,1)S(1)}, bf16[2,576]{1,0:T(2,128)(2,1)S(1)}, bf16[2,1152]{1,0:T(2,128)(2,1)S(1)}) all-reduce(bf16[2,6912]{1,0:T(2,128)(2,1)S(1)} %get-tuple-element.41, ...), channel_id=1, replica_groups=mesh['dp'=4,'tensor'=8] {'dp'}, use_global_device_ids=true, to_apply=%region_45.46 | all-reduce | flops 20160 | bytes 80640 | tf_op jit(solution)/shard_map/psum | solution.py:337
  1187.3 206.3 %all-reduce.5.cloned.1.call-done = (bf16[2,144,6912]{2,1,0:T(8,128)(2,1)}, bf16[2,1152,3,144]{1,3,2,0:T(8,128)(2,1)}, bf16[2,144,1152]{2,1,0:T(8,128)(2,1)}, bf1...) async-done(((bf16[2,144,6912]{2,1,0:T(8,128)(2,1)}, bf16[2,1152,3,144]{1,3,2,0:T(8,128)(2,1)}, bf16[2,144,1152]{2,1,0:T(8,128)(2,1)}, bf16[2,1152,576]{1,2,0:T(8,128)(2,1)}, ...) | async-done | bytes 11943952 | tf_op jit(solution)/shard_map/psum | solution.py:336
  1395.9 6.0 convert_element_type.432
  (517 shorter events, 220.1 us)
Async XLA Ops:
  7.2 181.5 %reduce-scatter.9.cloned.1.call-start = ((), (), s32[]{:S(2)}) async-start(), calls=%async_computation.8 | async-start | bytes 5308416 | tf_op jit(solution)/shard_map/reduce_scatter | solution.py:120
  9.1 98.4 %copy-start.71 = (f32[256]{0:T(256)}, f32[256]{0:T(256)S(1)}, u32[]{:S(2)}) copy-start(f32[256]{0:T(256)S(1)} %broadcast_multiply_fusion.3) | copy-start | bytes 3076
  10.5 97.0 %copy-start.77 = (f32[256]{0:T(256)}, f32[256]{0:T(256)S(1)}, u32[]{:S(2)}) copy-start(f32[256]{0:T(256)S(1)} %fusion.144) | copy-start | bytes 3076
  11.1 61.4 %copy-start.113 = (bf16[2,2,144]{2,1,0:T(2,128)(2,1)S(1)}, bf16[2,2,144]{2,1,0:T(2,128)(2,1)}, u32[]{:S(2)}) copy-start(bf16[2,2,144]{2,1,0:T(2,128)(2,1)} %param.18) | copy-start | bytes 3460
  11.1 75.6 %copy-start.31 = (bf16[2,1152,3,144]{1,3,2,0:T(8,128)(2,1)S(1)}, bf16[2,1152,3,144]{1,3,2,0:T(8,128)(2,1)}, u32[]{:S(2)}) copy-start(bf16[2,1152,3,144]{1,3,2,0:T(8,128)(2,1)} %param.17) | copy-start | bytes 5971972
  45.6 61.9 %copy-start.47 = (f32[1152]{0:T(1024)}, f32[1152]{0:T(1024)S(1)}, u32[]{:S(2)}) copy-start(f32[1152]{0:T(1024)S(1)} %get-tuple-element.33) | copy-start | bytes 13828
  45.6 146.0 %copy-start.57 = (f32[1152]{0:T(1024)}, f32[1152]{0:T(1024)S(1)}, u32[]{:S(2)}) copy-start(f32[1152]{0:T(1024)S(1)} %get-tuple-element.30) | copy-start | bytes 13828
  45.6 281.4 %copy-start.60 = (f32[1152]{0:T(1024)}, f32[1152]{0:T(1024)S(1)}, u32[]{:S(2)}) copy-start(f32[1152]{0:T(1024)S(1)} %get-tuple-element.31) | copy-start | bytes 13828
  45.6 340.8 %copy-start.49 = (f32[1152]{0:T(1024)}, f32[1152]{0:T(1024)S(1)}, u32[]{:S(2)}) copy-start(f32[1152]{0:T(1024)S(1)} %get-tuple-element.27) | copy-start | bytes 13828
  46.7 11.5 collective-permute-start
  58.2 14.3 %collective-permute-start.1 = (bf16[256,1152]{1,0:T(8,128)(2,1)S(1)}, bf16[256,1152]{1,0:T(8,128)(2,1)}, u32[]{:S(2)}, u32[]{:S(2)}) collective-permute-start(bf16[256,1152]{1,0:T(8,128)(2,1)S(1)} %collective-permute-done), channel_id=1, source_target_pairs={{0,1},{1,2},{2,3},{3,4},{4,5},{5,6},{6,7},{7,0},{8,9},{9,10},{10,1... | collective-permute-start | bytes 1769480 | tf_op jit(solution)/shard_map/ppermute | solution.py:27
  58.2 16.4 %collective-permute-start.4 = (bf16[256,1152]{1,0:T(8,128)(2,1)}, bf16[256,1152]{1,0:T(8,128)(2,1)}, u32[]{:S(2)}, u32[]{:S(2)}) collective-permute-start(bf16[256,1152]{1,0:T(8,128)(2,1)} %fusion.70), channel_id=1, source_target_pairs={{1,0},{2,1},{3,2},{4,3},{5,4},{6,5},{7,6},{0,7},{9,8},{10,9},{11,1... | collective-permute-start | bytes 1769480 | tf_op jit(solution)/shard_map/ppermute | solution.py:29
  72.5 14.2 %collective-permute-start.2 = (bf16[256,1152]{1,0:T(8,128)(2,1)}, bf16[256,1152]{1,0:T(8,128)(2,1)}, u32[]{:S(2)}, u32[]{:S(2)}) collective-permute-start(bf16[256,1152]{1,0:T(8,128)(2,1)} %collective-permute-done.1), channel_id=1, source_target_pairs={{0,1},{1,2},{2,3},{3,4},{4,5},{5,6},{6,7},{7,0},{8,9},{9,10},{10,1... | collective-permute-start | bytes 1769480 | tf_op jit(solution)/shard_map/ppermute | solution.py:27
  74.6 17.2 %collective-permute-start.5 = (bf16[256,1152]{1,0:T(8,128)(2,1)}, bf16[256,1152]{1,0:T(8,128)(2,1)S(1)}, u32[]{:S(2)}, u32[]{:S(2)}) collective-permute-start(bf16[256,1152]{1,0:T(8,128)(2,1)} %collective-permute-done.4), channel_id=1, source_target_pairs={{1,0},{2,1},{3,2},{4,3},{5,4},{6,5},{7,6},{0,7},{9,8},{10,9},{11,1... | collective-permute-start | bytes 1769480 | tf_op jit(solution)/shard_map/ppermute | solution.py:29
  86.7 15.2 %collective-permute-start.3 = (bf16[256,1152]{1,0:T(8,128)(2,1)}, bf16[256,1152]{1,0:T(8,128)(2,1)S(1)}, u32[]{:S(2)}, u32[]{:S(2)}) collective-permute-start(bf16[256,1152]{1,0:T(8,128)(2,1)} %collective-permute-done.2), channel_id=1, source_target_pairs={{0,1},{1,2},{2,3},{3,4},{4,5},{5,6},{6,7},{7,0},{8,9},{9,10},{10,1... | collective-permute-start | bytes 1769480 | tf_op jit(solution)/shard_map/ppermute | solution.py:27
  86.8 303.3 %copy-start.110 = (s32[1024]{0:T(1024)}, s32[1024]{0:T(1024)S(1)}, u32[]{:S(2)}) copy-start(s32[1024]{0:T(1024)S(1)} %pad_clamp_fusion) | copy-start | bytes 12292
  91.7 19.6 %collective-permute-start.6 = (bf16[256,1152]{1,0:T(8,128)(2,1)S(1)}, bf16[256,1152]{1,0:T(8,128)(2,1)S(1)}, u32[]{:S(2)}, u32[]{:S(2)}) collective-permute-start(bf16[256,1152]{1,0:T(8,128)(2,1)S(1)} %collective-permute-done.5), channel_id=1, source_target_pairs={{1,0},{2,1},{3,2},{4,3},{5,4},{6,5},{7,6},{0,7},{9,8},{10,9},{11,1... | collective-permute-start | bytes 1769480 | tf_op jit(solution)/shard_map/ppermute | solution.py:29
  135.3 191.7 %reduce-scatter.11.cloned.1.call-start = ((), (), s32[]{:S(2)}) async-start(), calls=%async_computation.9 | async-start | bytes 5308416 | tf_op jit(solution)/shard_map/reduce_scatter | solution.py:120
  190.1 57.6 %copy-start.79 = (f32[256]{0:T(256)}, f32[256]{0:T(256)S(1)}, u32[]{:S(2)}) copy-start(f32[256]{0:T(256)S(1)} %broadcast_multiply_fusion.2) | copy-start | bytes 3076
  191.6 57.8 %copy-start.106 = (f32[256]{0:T(256)}, f32[256]{0:T(256)S(1)}, u32[]{:S(2)}) copy-start(f32[256]{0:T(256)S(1)} %multiply_reduce_fusion.9) | copy-start | bytes 3076
  191.6 57.8 %copy-start.86 = (f32[256]{0:T(256)}, f32[256]{0:T(256)S(1)}, u32[]{:S(2)}) copy-start(f32[256]{0:T(256)S(1)} %fusion.145) | copy-start | bytes 3076
  192.0 11.2 collective-permute-start.7
  203.2 15.1 %collective-permute-start.8 = (bf16[256,1152]{1,0:T(8,128)(2,1)S(1)}, bf16[256,1152]{1,0:T(8,128)(2,1)S(1)}, u32[]{:S(2)}, u32[]{:S(2)}) collective-permute-start(bf16[256,1152]{1,0:T(8,128)(2,1)S(1)} %collective-permute-done.7), channel_id=1, source_target_pairs={{0,1},{1,2},{2,3},{3,4},{4,5},{5,6},{6,7},{7,0},{8,9},{9,10},{10,1... | collective-permute-start | bytes 1769480 | tf_op jit(solution)/shard_map/ppermute | solution.py:27
  203.2 15.6 %collective-permute-start.11 = (bf16[256,1152]{1,0:T(8,128)(2,1)S(1)}, bf16[256,1152]{1,0:T(8,128)(2,1)S(1)}, u32[]{:S(2)}, u32[]{:S(2)}) collective-permute-start(bf16[256,1152]{1,0:T(8,128)(2,1)S(1)} %add_convert_fusion.4), channel_id=1, source_target_pairs={{1,0},{2,1},{3,2},{4,3},{5,4},{6,5},{7,6},{0,7},{9,8},{10,9},{11,1... | collective-permute-start | bytes 1769480 | tf_op jit(solution)/shard_map/ppermute | solution.py:29
  218.3 13.8 collective-permute-start.9
  218.8 17.3 %collective-permute-start.12 = (bf16[256,1152]{1,0:T(8,128)(2,1)S(1)}, bf16[256,1152]{1,0:T(8,128)(2,1)S(1)}, u32[]{:S(2)}, u32[]{:S(2)}) collective-permute-start(bf16[256,1152]{1,0:T(8,128)(2,1)S(1)} %collective-permute-done.11), channel_id=1, source_target_pairs={{1,0},{2,1},{3,2},{4,3},{5,4},{6,5},{7,6},{0,7},{9,8},{10,9},{11,1... | collective-permute-start | bytes 1769480 | tf_op jit(solution)/shard_map/ppermute | solution.py:29
  232.1 14.6 %collective-permute-start.10 = (bf16[256,1152]{1,0:T(8,128)(2,1)S(1)}, bf16[256,1152]{1,0:T(8,128)(2,1)S(1)}, u32[]{:S(2)}, u32[]{:S(2)}) collective-permute-start(bf16[256,1152]{1,0:T(8,128)(2,1)S(1)} %collective-permute-done.9), channel_id=1, source_target_pairs={{0,1},{1,2},{2,3},{3,4},{4,5},{5,6},{6,7},{7,0},{8,9},{9,10},{10,1... | collective-permute-start | bytes 1769480 | tf_op jit(solution)/shard_map/ppermute | solution.py:27
  236.1 16.7 %collective-permute-start.13 = (bf16[256,1152]{1,0:T(8,128)(2,1)S(1)}, bf16[256,1152]{1,0:T(8,128)(2,1)S(1)}, u32[]{:S(2)}, u32[]{:S(2)}) collective-permute-start(bf16[256,1152]{1,0:T(8,128)(2,1)S(1)} %collective-permute-done.12), channel_id=1, source_target_pairs={{1,0},{2,1},{3,2},{4,3},{5,4},{6,5},{7,6},{0,7},{9,8},{10,9},{11,1... | collective-permute-start | bytes 1769480 | tf_op jit(solution)/shard_map/ppermute | solution.py:29
  273.8 204.0 %reduce-scatter.13.cloned.1.call-start = ((), (), s32[]{:S(2)}) async-start(), calls=%async_computation.10 | async-start | bytes 5308416 | tf_op jit(solution)/shard_map/reduce_scatter | solution.py:120
  328.5 57.9 %copy-start.69 = (f32[256]{0:T(256)}, f32[256]{0:T(256)S(1)}, u32[]{:S(2)}) copy-start(f32[256]{0:T(256)S(1)} %broadcast_multiply_fusion.1) | copy-start | bytes 3076
  328.8 56.8 %copy-start.108 = (f32[256]{0:T(256)}, f32[256]{0:T(256)S(1)}, u32[]{:S(2)}) copy-start(f32[256]{0:T(256)S(1)} %multiply_reduce_fusion.8) | copy-start | bytes 3076
  328.8 57.6 %copy-start.75 = (f32[256]{0:T(256)}, f32[256]{0:T(256)S(1)}, u32[]{:S(2)}) copy-start(f32[256]{0:T(256)S(1)} %fusion.146) | copy-start | bytes 3076
  329.1 11.2 collective-permute-start.14
  340.3 15.1 %collective-permute-start.15 = (bf16[256,1152]{1,0:T(8,128)(2,1)S(1)}, bf16[256,1152]{1,0:T(8,128)(2,1)S(1)}, u32[]{:S(2)}, u32[]{:S(2)}) collective-permute-start(bf16[256,1152]{1,0:T(8,128)(2,1)S(1)} %collective-permute-done.14), channel_id=1, source_target_pairs={{0,1},{1,2},{2,3},{3,4},{4,5},{5,6},{6,7},{7,0},{8,9},{9,10},{10,1... | collective-permute-start | bytes 1769480 | tf_op jit(solution)/shard_map/ppermute | solution.py:27
  340.3 15.6 %collective-permute-start.18 = (bf16[256,1152]{1,0:T(8,128)(2,1)S(1)}, bf16[256,1152]{1,0:T(8,128)(2,1)S(1)}, u32[]{:S(2)}, u32[]{:S(2)}) collective-permute-start(bf16[256,1152]{1,0:T(8,128)(2,1)S(1)} %add_convert_fusion.3), channel_id=1, source_target_pairs={{1,0},{2,1},{3,2},{4,3},{5,4},{6,5},{7,6},{0,7},{9,8},{10,9},{11,1... | collective-permute-start | bytes 1769480 | tf_op jit(solution)/shard_map/ppermute | solution.py:29
  355.4 13.8 collective-permute-start.16
  356.0 17.2 %collective-permute-start.19 = (bf16[256,1152]{1,0:T(8,128)(2,1)S(1)}, bf16[256,1152]{1,0:T(8,128)(2,1)S(1)}, u32[]{:S(2)}, u32[]{:S(2)}) collective-permute-start(bf16[256,1152]{1,0:T(8,128)(2,1)S(1)} %collective-permute-done.18), channel_id=1, source_target_pairs={{1,0},{2,1},{3,2},{4,3},{5,4},{6,5},{7,6},{0,7},{9,8},{10,9},{11,1... | collective-permute-start | bytes 1769480 | tf_op jit(solution)/shard_map/ppermute | solution.py:29
  369.2 13.7 collective-permute-start.17
  373.2 16.0 %collective-permute-start.20 = (bf16[256,1152]{1,0:T(8,128)(2,1)S(1)}, bf16[256,1152]{1,0:T(8,128)(2,1)S(1)}, u32[]{:S(2)}, u32[]{:S(2)}) collective-permute-start(bf16[256,1152]{1,0:T(8,128)(2,1)S(1)} %collective-permute-done.19), channel_id=1, source_target_pairs={{1,0},{2,1},{3,2},{4,3},{5,4},{6,5},{7,6},{0,7},{9,8},{10,9},{11,1... | collective-permute-start | bytes 1769480 | tf_op jit(solution)/shard_map/ppermute | solution.py:29
  424.5 165.7 %all-gather.5.cloned.1.call-start = ((), (), s32[]{:S(2)}) async-start(), calls=%async_computation.12 | async-start | bytes 5308416 | tf_op jit(solution)/shard_map/all_gather | solution.py:126
  427.1 236.6 %reduce-scatter.17.cloned.1.call-start = ((), (), s32[]{:S(2)}) async-start(), calls=%async_computation.13 | async-start | bytes 5308416 | tf_op jit(solution)/shard_map/reduce_scatter | solution.py:130
  479.1 92.4 %copy-start.73 = (f32[256]{0:T(256)}, f32[256]{0:T(256)S(1)}, u32[]{:S(2)}) copy-start(f32[256]{0:T(256)S(1)} %broadcast_multiply_fusion) | copy-start | bytes 3076
  479.4 92.2 %copy-start.81 = (f32[256]{0:T(256)}, f32[256]{0:T(256)S(1)}, u32[]{:S(2)}) copy-start(f32[256]{0:T(256)S(1)} %fusion.147) | copy-start | bytes 3076
  481.0 90.6 %copy-start.52 = (f32[1152]{0:T(1024)S(1)}, f32[1152]{0:T(1024)}, u32[]{:S(2)}) copy-start(f32[1152]{0:T(1024)} %get-tuple-element.25) | copy-start | bytes 13828
  481.0 90.6 %copy-start.66 = (f32[1152]{0:T(1024)S(1)}, f32[1152]{0:T(1024)}, u32[]{:S(2)}) copy-start(f32[1152]{0:T(1024)} %get-tuple-element.24) | copy-start | bytes 13828
  481.0 14.4 %collective-permute-start.21 = (bf16[256,1152]{1,0:T(8,128)(2,1)S(1)}, bf16[256,1152]{1,0:T(8,128)(2,1)S(1)}, u32[]{:S(2)}, u32[]{:S(2)}) collective-permute-start(bf16[256,1152]{1,0:T(8,128)(2,1)S(1)} %add_convert_fusion.2), channel_id=1, source_target_pairs={{0,1},{1,2},{2,3},{3,4},{4,5},{5,6},{6,7},{7,0},{8,9},{9,10},{10,1... | collective-permute-start | bytes 1769480 | tf_op jit(solution)/shard_map/ppermute | solution.py:27
  495.4 28.8 %collective-permute-start.22 = (bf16[256,1152]{1,0:T(8,128)(2,1)S(1)}, bf16[256,1152]{1,0:T(8,128)(2,1)S(1)}, u32[]{:S(2)}, u32[]{:S(2)}) collective-permute-start(bf16[256,1152]{1,0:T(8,128)(2,1)S(1)} %collective-permute-done.21), channel_id=1, source_target_pairs={{0,1},{1,2},{2,3},{3,4},{4,5},{5,6},{6,7},{7,0},{8,9},{9,10},{10,1... | collective-permute-start | bytes 1769480 | tf_op jit(solution)/shard_map/ppermute | solution.py:27
  495.4 28.9 %collective-permute-start.25 = (bf16[256,1152]{1,0:T(8,128)(2,1)S(1)}, bf16[256,1152]{1,0:T(8,128)(2,1)S(1)}, u32[]{:S(2)}, u32[]{:S(2)}) collective-permute-start(bf16[256,1152]{1,0:T(8,128)(2,1)S(1)} %add_convert_fusion.2), channel_id=1, source_target_pairs={{1,0},{2,1},{3,2},{4,3},{5,4},{6,5},{7,6},{0,7},{9,8},{10,9},{11,1... | collective-permute-start | bytes 1769480 | tf_op jit(solution)/shard_map/ppermute | solution.py:29
  524.2 26.7 %collective-permute-start.23 = (bf16[256,1152]{1,0:T(8,128)(2,1)S(1)}, bf16[256,1152]{1,0:T(8,128)(2,1)S(1)}, u32[]{:S(2)}, u32[]{:S(2)}) collective-permute-start(bf16[256,1152]{1,0:T(8,128)(2,1)S(1)} %collective-permute-done.22), channel_id=1, source_target_pairs={{0,1},{1,2},{2,3},{3,4},{4,5},{5,6},{6,7},{7,0},{8,9},{9,10},{10,1... | collective-permute-start | bytes 1769480 | tf_op jit(solution)/shard_map/ppermute | solution.py:27
  524.2 28.8 %collective-permute-start.26 = (bf16[256,1152]{1,0:T(8,128)(2,1)S(1)}, bf16[256,1152]{1,0:T(8,128)(2,1)S(1)}, u32[]{:S(2)}, u32[]{:S(2)}) collective-permute-start(bf16[256,1152]{1,0:T(8,128)(2,1)S(1)} %collective-permute-done.25), channel_id=1, source_target_pairs={{1,0},{2,1},{3,2},{4,3},{5,4},{6,5},{7,6},{0,7},{9,8},{10,9},{11,1... | collective-permute-start | bytes 1769480 | tf_op jit(solution)/shard_map/ppermute | solution.py:29
  550.9 17.2 %collective-permute-start.24 = (bf16[256,1152]{1,0:T(8,128)(2,1)S(1)}, bf16[256,1152]{1,0:T(8,128)(2,1)S(1)}, u32[]{:S(2)}, u32[]{:S(2)}) collective-permute-start(bf16[256,1152]{1,0:T(8,128)(2,1)S(1)} %collective-permute-done.23), channel_id=1, source_target_pairs={{0,1},{1,2},{2,3},{3,4},{4,5},{5,6},{6,7},{7,0},{8,9},{9,10},{10,1... | collective-permute-start | bytes 1769480 | tf_op jit(solution)/shard_map/ppermute | solution.py:27
  553.0 22.5 %collective-permute-start.27 = (bf16[256,1152]{1,0:T(8,128)(2,1)S(1)}, bf16[256,1152]{1,0:T(8,128)(2,1)S(1)}, u32[]{:S(2)}, u32[]{:S(2)}) collective-permute-start(bf16[256,1152]{1,0:T(8,128)(2,1)S(1)} %collective-permute-done.26), channel_id=1, source_target_pairs={{1,0},{2,1},{3,2},{4,3},{5,4},{6,5},{7,6},{0,7},{9,8},{10,9},{11,1... | collective-permute-start | bytes 1769480 | tf_op jit(solution)/shard_map/ppermute | solution.py:29
  607.3 111.9 %reduce-scatter.15.cloned.1.call-start = ((), (), s32[]{:S(2)}) async-start(), calls=%async_computation.11 | async-start | bytes 5308416 | tf_op jit(solution)/shard_map/reduce_scatter | solution.py:120
  617.5 157.5 %all-gather.7.cloned.1.call-start = ((), (), s32[]{:S(2)}) async-start(), calls=%async_computation.14 | async-start | bytes 5308416 | tf_op jit(solution)/shard_map/all_gather | solution.py:126
  724.7 135.7 %reduce-scatter.19.cloned.1.call-start = ((), (), s32[]{:S(2)}) async-start(), calls=%async_computation.15 | async-start | bytes 5308416 | tf_op jit(solution)/shard_map/reduce_scatter | solution.py:130
  806.5 58.3 %copy-start.3 = (f32[256,1152]{1,0:T(8,128)S(1)}, f32[256,1152]{1,0:T(8,128)}, u32[]{:S(2)}) copy-start(f32[256,1152]{1,0:T(8,128)} %copy-done.2) | copy-start | bytes 3538948
  806.5 111.1 %all-gather.9.cloned.1.call-start = ((), (), s32[]{:S(2)}) async-start(), calls=%async_computation.16 | async-start | bytes 5308416 | tf_op jit(solution)/shard_map/all_gather | solution.py:126
  867.4 121.2 %reduce-scatter.21.cloned.1.call-start = ((), (), s32[]{:S(2)}) async-start(), calls=%async_computation.17 | async-start | bytes 5308416 | tf_op jit(solution)/shard_map/reduce_scatter | solution.py:130
  934.6 56.3 %copy-start.107 = (f32[256]{0:T(256)S(1)}, f32[256]{0:T(256)}, u32[]{:S(2)}) copy-start(f32[256]{0:T(256)} %copy-done.106) | copy-start | bytes 3076
  934.7 56.9 %copy-start.7 = (f32[256,1152]{1,0:T(8,128)S(1)}, f32[256,1152]{1,0:T(8,128)}, u32[]{:S(2)}) copy-start(f32[256,1152]{1,0:T(8,128)} %get-tuple-element.58) | copy-start | bytes 3538948
  934.7 109.3 %all-gather.11.cloned.1.call-start = ((), (), s32[]{:S(2)}) async-start(), calls=%async_computation.18 | async-start | bytes 5308416 | tf_op jit(solution)/shard_map/all_gather | solution.py:126
  993.7 54.5 %copy-start.68 = (f32[8,2,256]{2,1,0:T(2,128)S(1)}, f32[8,2,256]{2,1,0:T(2,128)}, u32[]{:S(2)}) copy-start(f32[8,2,256]{2,1,0:T(2,128)} %copy-done.67) | copy-start | bytes 49156
  993.7 131.0 %reduce-scatter.23.cloned.1.call-start = ((), (), s32[]{:S(2)}) async-start(), calls=%async_computation.19 | async-start | bytes 5308416 | tf_op jit(solution)/shard_map/reduce_scatter | solution.py:130
  1060.9 332.7 %all-reduce.5.cloned.1.call-start = ((), (), s32[]{:S(2)}) async-start(), calls=%async_computation.20 | async-start | bytes 23887872 | tf_op jit(solution)/shard_map/psum | solution.py:336
  (107 other events, 903.7 us)
Sparse Core Ops, SparseCore 0:
  135.5 53.1 reduce-scatter.8
  273.9 53.0 reduce-scatter.10
  424.7 53.0 reduce-scatter.12
  479.8 73.1 all-gather.4
  607.5 56.2 reduce-scatter.16
  665.9 53.2 reduce-scatter.14
  724.8 50.0 all-gather.6
  806.6 53.7 reduce-scatter.18
  867.5 50.0 all-gather.8
  934.8 53.7 reduce-scatter.20
  993.8 50.0 all-gather.10
  1061.0 53.7 reduce-scatter.22
  1161.2 232.3 all-reduce.4
